TPU v7x, 128 devices: a whole 4x4x4 slice. The times are simulated.
128 devices in a mesh: row: 8 (over z_lo, y), col: 16 (over z_hi, x, core).
Axes of the slice: x: 4, y: 4, z: 4 (z_hi: 2, z_lo: 2; z = z_hi * 2 + z_lo), core: 2. Of those that a mesh axis runs over, the one named last changes fastest.
Arguments:
- front: float32 [16384, 16384], P('row', 'col'), as said below
- child_updates: bfloat16 [8, 4096, 4096], P('row', 'col'), as said below
- child_maps: int32 [8, 16], replicated, may hold values from 0 to 63, as said below
- fill_mask: int32 [64, 64], replicated, may hold values from 0 to 1, as said below
Outputs:
- factored: float32 [16384, 16384], P('row', 'col')
Inputs may be any that keep to these rules, and one draw needn't show every extreme that they name: front is symmetric. `child_updates`: each child's matrix is symmetric. `child_maps`: each row lists 16 distinct block indices in ascending order; in every aligned run of 4 indices a row names at most 2, and exactly 2 in some run; in every aligned run of 8 indices at most 4, and exactly 4 in some run. `fill_mask`: symmetric, ones on the diagonal.
All inputs are finite; a program needn't handle non-finite values.
Results may differ from a plain program's by a relative error of at most 0.0003.
Values may be sent and summed in bfloat16 or wider, within the bound.
A program may use at most 192 MiB of HBM per device.

v0:
```python
import jax
import jax.numpy as jnp
from jax import lax
from jax.sharding import PartitionSpec as P

BS = 256
CB = 16
PB = 2
STEPS = 2


def broadcast(shard, axis, root):
    mine = lax.axis_index(axis) == root
    return lax.psum(jnp.where(mine, shard, jnp.zeros_like(shard)), axis)


def span_ranks(spans):
    items_count = spans.shape[-1]
    agrees = spans[..., :, None] == spans[..., None, :]
    earlier = jnp.arange(items_count)[None, :] < jnp.arange(items_count)[:, None]
    return jnp.sum(agrees & earlier, axis=-1)


def one_hot_slots(spans, ranks, slot_groups, slot_depth):
    matches = (spans[None, None, :] == jnp.arange(slot_groups)[:, None, None]) & (
        ranks[None, None, :] == jnp.arange(slot_depth)[None, :, None]
    )
    return matches.astype(jnp.bfloat16)


def placement(block_map, span_index, per_span, slot_depth):
    spans = block_map // per_span
    ranks = span_ranks(spans)
    local_block = block_map - span_index * per_span
    matches = (
        (spans[:, None, None, :] == span_index)
        & (ranks[:, None, None, :] == jnp.arange(slot_depth)[None, None, :, None])
        & (local_block[:, None, None, :] == jnp.arange(per_span)[None, :, None, None])
    )
    return jnp.sum(matches.astype(jnp.int32), axis=-1).astype(jnp.bfloat16)


def triangular(factor, panel_rows):
    return jax.scipy.linalg.solve_triangular(factor, panel_rows.T, lower=True).T


def pivot_of(panel_rows, row_owner, row_at, panel_width):
    return broadcast(panel_rows[row_at : row_at + panel_width], "row", row_owner)


def local(front, child_updates, child_maps, fill_mask):
    row_len, col_len = front.shape
    n_row = lax.axis_size("row")
    n_col = lax.axis_size("col")
    row_me = lax.axis_index("row")
    col_me = lax.axis_index("col")
    edge_len = BS
    row_blocks = row_len // edge_len
    col_blocks = col_len // edge_len
    depth_col = 2
    depth_row = 2 * (n_col // n_row)
    panel_width = PB * BS
    own_map = lax.dynamic_index_in_dim(child_maps, row_me, 0, keepdims=False)
    col_spans = own_map // col_blocks
    pack_cols = one_hot_slots(col_spans, span_ranks(col_spans), n_col, depth_col)
    updates = child_updates[0]
    local_rows = updates.shape[0]
    tiles_grid = updates.reshape(local_rows, CB, edge_len)
    packed = jnp.einsum(
        "jtb,xby->jxty", pack_cols, tiles_grid, preferred_element_type=jnp.float32
    ).astype(jnp.bfloat16)
    packed = packed.reshape(n_col, local_rows, depth_col * edge_len)
    gathered = lax.all_to_all(packed, "col", split_axis=0, concat_axis=0, tiled=True)
    row_spans = own_map // row_blocks
    pack_rows = one_hot_slots(row_spans, span_ranks(row_spans), n_row, depth_row)
    packed_two = jnp.einsum(
        "rsa,axz->rsxz", pack_rows, gathered, preferred_element_type=jnp.float32
    ).astype(jnp.bfloat16)
    packed_two = packed_two.reshape(n_row, depth_row * edge_len, depth_col * edge_len)
    arrived = lax.all_to_all(packed_two, "row", split_axis=0, concat_axis=0, tiled=True)
    arrived = arrived.reshape(n_row, depth_row, edge_len, depth_col * edge_len)
    rows_place = placement(child_maps, row_me, row_blocks, depth_row)
    cols_place = placement(child_maps, col_me, col_blocks, depth_col)
    placed = jnp.einsum(
        "kis,ksxz->kixz", rows_place, arrived, preferred_element_type=jnp.float32
    ).astype(jnp.bfloat16)
    placed = placed.reshape(n_row, row_blocks, edge_len, depth_col, edge_len)
    assembled = jnp.einsum(
        "kixty,kjt->ixjy", placed, cols_place, preferred_element_type=jnp.float32
    )
    mask_local = lax.dynamic_slice(
        fill_mask, (row_me * row_blocks, col_me * col_blocks), (row_blocks, col_blocks)
    ).astype(jnp.float32)
    mask_full = jnp.broadcast_to(
        mask_local[:, None, :, None], (row_blocks, edge_len, col_blocks, edge_len)
    ).reshape(row_len, col_len)
    working = (front + assembled.reshape(row_len, col_len)) * mask_full
    global_rows = row_me * row_len + jnp.arange(row_len)
    global_cols = col_me * col_len + jnp.arange(col_len)
    lower_blocks = global_rows[:, None] // edge_len >= global_cols[None, :] // edge_len
    source_row = col_me * col_len // row_len
    source_offset = col_me * col_len % row_len
    for step_index in range(STEPS):
        first_col = step_index * panel_width
        finish = first_col + panel_width
        col_owner = first_col // col_len
        col_at = first_col % col_len
        row_owner = first_col // row_len
        row_at = first_col % row_len
        panel_local = working[:, col_at : col_at + panel_width]
        pivot_rows = (global_rows >= first_col) & (global_rows < finish)
        factor = jnp.linalg.cholesky(pivot_of(panel_local, row_owner, row_at, panel_width))
        factor_padded = lax.dynamic_update_slice_in_dim(
            jnp.zeros((row_len, panel_width), jnp.float32), factor, row_at, 0
        )
        solved = jnp.where(pivot_rows[:, None], factor_padded, triangular(factor, panel_local))
        rows_factor = broadcast(solved, "col", col_owner)
        picked = lax.dynamic_slice_in_dim(rows_factor, source_offset, col_len, 0)
        cols_factor = broadcast(picked.astype(jnp.bfloat16), "row", source_row).astype(picked.dtype)
        product = jnp.dot(
            rows_factor,
            cols_factor.T,
            precision=lax.Precision.HIGHEST,
            preferred_element_type=jnp.float32,
        )
        trailing = (global_cols >= finish)[None, :]
        working = jnp.where(trailing, working - product * mask_full, working)
        current = working[:, col_at : col_at + panel_width]
        panel_now = jnp.where(col_me == col_owner, rows_factor, current)
        working = lax.dynamic_update_slice_in_dim(working, panel_now, col_at, 1)
    return jnp.where(lower_blocks, working, 0.0)


def solution(mesh):
    placed = (P("row", "col"), P("row", "col", None), P(), P())
    return jax.shard_map(
        local, mesh=mesh, in_specs=placed, out_specs=P("row", "col"), check_vma=False
    )
```

profile of v0, /device:TPU:0, one launch (start us, length us, event | category | flops | bytes accessed | tf_op | source)
XLA Modules:
  0.0 1288.0 jit_solution(16817608450089591911)
XLA Ops:
  34.9 56.1 %all-to-all-done = bf16[16,256,512]{2,1,0:T(8,128)(2,1)} async-done(((bf16[16,256,512]{2,1,0:T(8,128)(2,1)}), bf16[16,256,512]{2,1,0:T(8,128)(2,1)}, u32[]{:S(2)}, u32[]{:S(2)}) %all-to-all-start) | async-done | bytes 4194336 | tf_op jit(solution)/shard_map/all_to_all | solution.py:73
  99.6 9.5 copy.92
  123.4 9.2 copy.97
  134.0 74.9 %all-to-all-done.1 = bf16[8,1024,512]{2,1,0:T(8,128)(2,1)} async-done(((bf16[8,1024,512]{2,1,0:T(8,128)(2,1)}), bf16[8,1024,512]{2,1,0:T(8,128)(2,1)}, u32[]{:S(2)}, u32[]{:S(2)}) %all-to-all-start.1) | async-done | bytes 8388640 | tf_op jit(solution)/shard_map/all_to_all | solution.py:80
  208.9 13.9 %convolution_convert_fusion = bf16[8,8,256,512]{3,1,2,0:T(8,128)(2,1)} fusion(bf16[8,4,256,512]{3,2,1,0:T(8,128)(2,1)} %bitcast.14, s32[8,8,4]{1,2,0:T(4,128)S(1)} %convert_reduce_fusion), kind=kOutput, calls=%fused_computation.8 | convolution fusion | flops 75497728 | bytes 25166848 | tf_op jit(solution)/shard_map/kis,ksxz->kixz/dot_general | solution.py:84
  222.8 30.2 %fusion = f32[4,8,256,256,1]{3,0,4,2,1:T(4,128)} fusion(bf16[8,8,256,2,256]{4,1,3,2,0:T(8,128)(2,1)} %bitcast.176, bf16[8,4,2,1,1]{0,2,1,4,3:T(2,128)(2,1)S(1)} %convert_bitcast_fusion.1), kind=kOutput, calls=%fused_computation.4 | convolution fusion | flops 67108864 | bytes 25165952 | tf_op jit(solution)/shard_map/kixty,kjt->ixjy/dot_general | solution.py:88
  270.7 9.6 add_multiply_fusion
  289.4 103.7 %all-reduce.10.cloned.1.call-done = f32[512,512]{0,1:T(8,128)} async-done(((f32[512,512]{0,1:T(8,128)}), f32[512,512]{0,1:T(8,128)}) %all-reduce.10.cloned.1.call-update) | async-done | bytes 1048592 | tf_op jit(solution)/shard_map/psum | solution.py:14
  396.1 11.7 cholesky.286
  407.8 9.8 custom-call.27
  418.3 11.7 cholesky.305
  430.4 10.2 custom-call.28
  441.7 11.7 cholesky.326
  453.6 9.8 custom-call.29
  464.2 11.9 cholesky.343
  489.8 39.3 %custom-call.30 = f32[4,128,128]{1,2,0:T(8,128)S(1)} custom-call(f32[4,128,128]{2,1,0:T(8,128)S(1)} %get-tuple-element.21), custom_call_target="InvertDiagBlocksLowerTriangular" | custom-call | tf_op jit(solution)/shard_map/jit(_solve_triangular)/triangular_solve | solution.py:44
  543.0 150.2 %all-reduce.12.cloned.1.call-done = f32[2048,512]{0,1:T(8,128)} async-done(((f32[2048,512]{0,1:T(8,128)}), f32[2048,512]{0,1:T(8,128)}) %all-reduce.12.cloned.1.call-update) | async-done | bytes 4194320 | tf_op jit(solution)/shard_map/psum | solution.py:14
  696.1 77.9 %all-reduce.14.cloned.1.call-done = bf16[1024,512]{0,1:T(8,128)(2,1)} async-done(((bf16[1024,512]{0,1:T(8,128)(2,1)}), bf16[1024,512]{0,1:T(8,128)(2,1)}) %all-reduce.14.cloned.1.call-update) | async-done | bytes 1048592 | tf_op jit(solution)/shard_map/psum | solution.py:14
  774.0 14.3 %subtract_select_fusion.1 = f32[2048,1024]{0,1:T(8,128)S(1)} fusion(f32[2048,1024]{0,1:T(8,128)} %copy-done.1, f32[2048,1024]{0,1:T(8,128)} %bitcast.174, f32[2048,512]{0,1:T(8,128)} %all-reduce.12.cloned.1.call-done, bf16[1024,512]{0,1:T(8,128)(2,1)} %all-reduce.14.cloned.1.call-done, pred[1024]{0:T(1024)(128)(4,1)S(1)} %fusion.104), kind=kOutput, calls=%fused_computation.7 | convolution fusion | flops 12891193344 | bytes 30409728 | tf_op jit(solution)/shard_map/dot_general | solution.py:120
  798.7 72.1 %all-reduce.16.cloned.1.call-done = f32[512,512]{0,1:T(8,128)} async-done(((f32[512,512]{0,1:T(8,128)}), f32[512,512]{0,1:T(8,128)}) %all-reduce.16.cloned.1.call-update) | async-done | bytes 1048592 | tf_op jit(solution)/shard_map/psum | solution.py:14
  873.8 11.7 cholesky.358
  885.5 9.8 custom-call.31
  896.0 11.7 cholesky.377
  908.1 10.0 custom-call.32
  919.2 11.7 cholesky.398
  931.0 9.8 custom-call.33
  941.6 11.9 cholesky.415
  968.0 39.3 %custom-call.34 = f32[4,128,128]{1,2,0:T(8,128)S(1)} custom-call(f32[4,128,128]{2,1,0:T(8,128)S(1)} %get-tuple-element.22), custom_call_target="InvertDiagBlocksLowerTriangular" | custom-call | tf_op jit(solution)/shard_map/jit(_solve_triangular)/triangular_solve | solution.py:44
  1021.1 150.2 %all-reduce.18.cloned.1.call-done = f32[2048,512]{0,1:T(8,128)} async-done(((f32[2048,512]{0,1:T(8,128)}), f32[2048,512]{0,1:T(8,128)}) %all-reduce.18.cloned.1.call-update) | async-done | bytes 4194320 | tf_op jit(solution)/shard_map/psum | solution.py:14
  1174.3 77.9 %all-reduce.20.cloned.1.call-done = bf16[1024,512]{0,1:T(8,128)(2,1)} async-done(((bf16[1024,512]{0,1:T(8,128)(2,1)}), bf16[1024,512]{0,1:T(8,128)(2,1)}) %all-reduce.20.cloned.1.call-update) | async-done | bytes 1048592 | tf_op jit(solution)/shard_map/psum | solution.py:14
  1252.2 14.1 %subtract_select_fusion = f32[2048,1024]{0,1:T(8,128)S(1)} fusion(f32[2048,1024]{0,1:T(8,128)} %copy-done, f32[2048,1024]{0,1:T(8,128)} %bitcast.175, f32[2048,512]{0,1:T(8,128)} %all-reduce.18.cloned.1.call-done, bf16[1024,512]{0,1:T(8,128)(2,1)} %all-reduce.20.cloned.1.call-done, pred[1024]{0:T(1024)(128)(4,1)S(1)} %fusion.103), kind=kOutput, calls=%fused_computation.6 | convolution fusion | flops 12891193344 | bytes 30409728 | tf_op jit(solution)/shard_map/dot_general | solution.py:120
  1271.5 9.2 copy.119
  (195 shorter events, 180.1 us)
Async XLA Ops:
  26.9 64.2 %all-to-all-start = ((bf16[16,256,512]{2,1,0:T(8,128)(2,1)}), bf16[16,256,512]{2,1,0:T(8,128)(2,1)}, u32[]{:S(2)}, u32[]{:S(2)}) async-start(bf16[16,256,512]{2,1,0:T(8,128)(2,1)} %copy.90), calls=%async_computation | async-start | bytes 8388608 | tf_op jit(solution)/shard_map/all_to_all | solution.py:73
  109.1 99.8 %all-to-all-start.1 = ((bf16[8,1024,512]{2,1,0:T(8,128)(2,1)}), bf16[8,1024,512]{2,1,0:T(8,128)(2,1)}, u32[]{:S(2)}, u32[]{:S(2)}) async-start(bf16[8,1024,512]{2,1,0:T(8,128)(2,1)} %copy.92), calls=%async_computation.1 | async-start | bytes 16777216 | tf_op jit(solution)/shard_map/all_to_all | solution.py:80
  114.1 278.9 %all-reduce.10.cloned.1.call-start = ((), (), s32[]{:S(2)}) async-start(), calls=%async_computation.2 | async-start | bytes 2097152 | tf_op jit(solution)/shard_map/psum | solution.py:14
  123.4 9.2 copy-start.6
  280.3 3.2 copy-start.1
  284.7 408.5 %all-reduce.12.cloned.1.call-start = ((), (), s32[]{:S(2)}) async-start(), calls=%async_computation.3 | async-start | bytes 8388608 | tf_op jit(solution)/shard_map/psum | solution.py:14
  529.1 5.8 copy-start.4
  542.9 231.1 %all-reduce.14.cloned.1.call-start = ((), (), s32[]{:S(2)}) async-start(), calls=%async_computation.4 | async-start | bytes 2097152 | tf_op jit(solution)/shard_map/psum | solution.py:14
  696.0 174.7 %all-reduce.16.cloned.1.call-start = ((), (), s32[]{:S(2)}) async-start(), calls=%async_computation.5 | async-start | bytes 2097152 | tf_op jit(solution)/shard_map/psum | solution.py:14
  774.0 14.3 %copy-start.2 = (f32[2048,512]{0,1:T(8,128)S(1)}, f32[2048,512]{0,1:T(8,128)}, u32[]{:S(2)}) copy-start(f32[2048,512]{0,1:T(8,128)} %all-reduce.12.cloned.1.call-done) | copy-start | bytes 12582916
  789.6 3.2 copy-start
  793.9 377.4 %all-reduce.18.cloned.1.call-start = ((), (), s32[]{:S(2)}) async-start(), calls=%async_computation.6 | async-start | bytes 8388608 | tf_op jit(solution)/shard_map/psum | solution.py:14
  1007.3 5.8 copy-start.5
  1021.1 231.1 %all-reduce.20.cloned.1.call-start = ((), (), s32[]{:S(2)}) async-start(), calls=%async_computation.7 | async-start | bytes 2097152 | tf_op jit(solution)/shard_map/psum | solution.py:14
  1252.2 14.1 %copy-start.3 = (f32[2048,512]{0,1:T(8,128)S(1)}, f32[2048,512]{0,1:T(8,128)}, u32[]{:S(2)}) copy-start(f32[2048,512]{0,1:T(8,128)} %all-reduce.18.cloned.1.call-done) | copy-start | bytes 12582916
Sparse Core Ops, SparseCore 0:
  284.8 108.2 all-reduce.9
  543.0 150.1 all-reduce.11
  696.2 77.7 all-reduce.13
  794.0 76.6 all-reduce.15
  1021.2 150.1 all-reduce.17
  1174.3 77.7 all-reduce.19
where the time goes:
time: 1300 us; the launch traced here: 1290 us
  waiting for transfers between devices  763 us (59%)
  other arithmetic  273 us (21%)
  matrix products  111 us (9%)
  local copies, waits for them, and re-layouts  107 us (8%)
  between operations  19.9 us (2%)
  starting transfers between devices  13.4 us (1%)
    psum x6, waiting for transfers between devices, broadcast(): return lax.psum(jnp.where(mine, shard, jnp.zeros_like(shard)), axis)  632 us
    another operation x29, other arithmetic, local(): jnp.linalg.cholesky(pivot_of(panel_local, row_owner, row_at, panel_width))  159 us
    another operation x5, other arithmetic, triangular(): return jax.scipy.linalg.solve_triangular(factor, panel_rows.T, lower=True).T  79.1 us
    all_to_all x1, waiting for transfers between devices, local(): lax.all_to_all(packed_two, 'row', split_axis=0, concat_axis=0, tiled=True)  74.9 us
    all_to_all x1, waiting for transfers between devices, local(): lax.all_to_all(packed, 'col', split_axis=0, concat_axis=0, tiled=True)  56.1 us
    unnamed x18, local copies, waits for them, and re-layouts  34 us
    dot_general x1, matrix products, local(): jnp.einsum('kixty,kjt->ixjy', placed, cols_place, preferred_element_type=...  30.2 us
    dot_general x2, matrix products, local(): jnp.dot(rows_factor, cols_factor.T, precision=lax.Precision.HIGHEST, pref...  28.4 us
  transfers between devices with their start and end apart: 8, of which 8 were waited for; matrix products, arithmetic and copies ran while one was open for 2% of the time, Pallas kernels for 0%

commit v1 on v0

--- a/solution.py
+++ b/solution.py
@@ -11,7 +11,7 @@
 
 def broadcast(shard, axis, root):
     mine = lax.axis_index(axis) == root
-    return lax.psum(jnp.where(mine, shard, jnp.zeros_like(shard)), axis)
+    return jnp.sum(lax.all_gather(jnp.where(mine, shard, jnp.zeros_like(shard)), axis), axis=0)
 
 
 def span_ranks(spans):

time: 1300 us -> 1800 us (1.38)
  waiting for transfers between devices: 763 us -> 1210 us
  other arithmetic: 273 us -> 338 us
  local copies, waits for them, and re-layouts: 107 us -> 81.3 us
  matrix products: 111 us -> 130 us
    all_gather x0 -> x6, waiting for transfers between devices: none -> 1070 us  [broadcast(): lax.all_gather(jnp.where(mine, shard, jnp.zeros_like(shard)), axis)]
    psum x6 -> x0, waiting for transfers between devices: 632 us -> none  [broadcast(): return lax.psum(jnp.where(mine, shard, jnp.zeros_like(shard)), axis)]
    reduce_sum x0 -> x6, other arithmetic: none -> 65.6 us  [broadcast(): jnp.sum(lax.all_gather(jnp.where(mine, shard, jnp.zeros_like(shard)), axi...]
  transfers between devices with their start and end apart: 8 -> 8, of which waited for: 8 -> 8; matrix products, arithmetic and copies ran while one was open for 2% -> 1% of each run, Pallas kernels for 0% -> 0%
where the time goes in v1:
time: 1800 us; the launch traced here: 1790 us
  waiting for transfers between devices  1210 us (67%)
  other arithmetic  338 us (19%)
  matrix products  130 us (7%)
  local copies, waits for them, and re-layouts  81.3 us (5%)
  between operations  19.6 us (1%)
    all_gather x6, waiting for transfers between devices, broadcast(): lax.all_gather(jnp.where(mine, shard, jnp.zeros_like(shard)), axis)  1070 us
    another operation x29, other arithmetic, local(): jnp.linalg.cholesky(pivot_of(panel_local, row_owner, row_at, panel_width))  159 us
    all_to_all x1, waiting for transfers between devices, local(): lax.all_to_all(packed_two, 'row', split_axis=0, concat_axis=0, tiled=True)  85.6 us
    another operation x5, other arithmetic, triangular(): return jax.scipy.linalg.solve_triangular(factor, panel_rows.T, lower=True).T  81.1 us
    reduce_sum x6, other arithmetic, broadcast(): jnp.sum(lax.all_gather(jnp.where(mine, shard, jnp.zeros_like(shard)), axi...  65.6 us
    all_to_all x1, waiting for transfers between devices, local(): lax.all_to_all(packed, 'col', split_axis=0, concat_axis=0, tiled=True)  56.1 us
    another operation x14, matrix products, triangular(): return jax.scipy.linalg.solve_triangular(factor, panel_rows.T, lower=True).T  39 us
  transfers between devices with their start and end apart: 8, of which 8 were waited for; matrix products, arithmetic and copies ran while one was open for 1% of the time, Pallas kernels for 0%

profile of v1, /device:TPU:0, one launch (start us, length us, event | category | flops | bytes accessed | tf_op | source)
XLA Modules:
  0.0 1790.1 jit_solution(1515600992279054137)
XLA Ops:
  34.9 56.1 %all-to-all-done = bf16[16,256,512]{2,1,0:T(8,128)(2,1)} async-done(((bf16[16,256,512]{2,1,0:T(8,128)(2,1)}), bf16[16,256,512]{2,1,0:T(8,128)(2,1)}, u32[]{:S(2)}, u32[]{:S(2)}) %all-to-all-start) | async-done | bytes 4194336 | tf_op jit(solution)/shard_map/all_to_all | solution.py:73
  99.6 9.5 copy.56
  123.2 85.6 %all-to-all-done.1 = bf16[8,1024,512]{2,1,0:T(8,128)(2,1)} async-done(((bf16[8,1024,512]{2,1,0:T(8,128)(2,1)}), bf16[8,1024,512]{2,1,0:T(8,128)(2,1)}, u32[]{:S(2)}, u32[]{:S(2)}) %all-to-all-start.1) | async-done | bytes 8388640 | tf_op jit(solution)/shard_map/all_to_all | solution.py:80
  208.8 13.9 convolution_convert_fusion
  222.7 30.1 %fusion = f32[4,8,256,256,1]{3,0,4,2,1:T(4,128)} fusion(bf16[8,8,256,2,256]{4,1,3,2,0:T(8,128)(2,1)} %bitcast.186, bf16[8,4,2,1,1]{0,2,1,4,3:T(2,128)(2,1)S(1)} %convert_bitcast_fusion.1), kind=kOutput, calls=%fused_computation.4 | convolution fusion | flops 67108864 | bytes 25165952 | tf_op jit(solution)/shard_map/kixty,kjt->ixjy/dot_general | solution.py:88
  252.8 8.9 copy.92
  278.2 118.6 %all-gather.13.cloned.1.call-done = f32[4096,512]{1,0:T(8,128)} async-done(((f32[512,512]{1,0:T(8,128)}), f32[4096,512]{1,0:T(8,128)}) %all-gather.13.cloned.1.call-update) | async-done | bytes 8388624 | tf_op jit(solution)/shard_map/all_gather | solution.py:14
  402.0 11.7 cholesky.286
  413.8 9.8 custom-call.27
  424.3 12.1 cholesky.305
  436.4 9.8 custom-call.28
  446.9 11.7 cholesky.326
  459.3 9.8 custom-call.29
  469.7 11.9 cholesky.343
  494.3 39.3 %custom-call.30 = f32[4,128,128]{1,2,0:T(8,128)S(1)} custom-call(f32[4,128,128]{2,1,0:T(8,128)S(1)} %get-tuple-element.21), custom_call_target="InvertDiagBlocksLowerTriangular" | custom-call | tf_op jit(solution)/shard_map/jit(_solve_triangular)/triangular_solve | solution.py:44
  561.1 341.3 %all-gather.15.cloned.1.call-done = f32[32768,512]{1,0:T(8,128)} async-done(((f32[2048,512]{1,0:T(8,128)}), f32[32768,512]{1,0:T(8,128)}) %all-gather.15.cloned.1.call-update) | async-done | bytes 67108880 | tf_op jit(solution)/shard_map/all_gather | solution.py:14
  902.4 23.1 %reduce_sum.121 = f32[2048,512]{1,0:T(8,128)} reduce(f32[16,2048,512]{2,1,0:T(8,128)} %bitcast.33, f32[]{:T(128)} %constant.221.clone.1), dimensions={0}, to_apply=%region_15.18 | reduce | flops 15728640 | bytes 71303168 | tf_op jit(solution)/shard_map/reduce_sum | solution.py:14
  928.5 89.2 %all-gather.17.cloned.1.call-done = bf16[8192,512]{1,0:T(8,128)(2,1)} async-done(((bf16[1024,512]{1,0:T(8,128)(2,1)}), bf16[8192,512]{1,0:T(8,128)(2,1)}) %all-gather.17.cloned.1.call-update) | async-done | bytes 8388624 | tf_op jit(solution)/shard_map/all_gather | solution.py:14
  1022.9 15.7 subtract_select_fusion.1
  1049.1 86.0 %all-gather.19.cloned.1.call-done = f32[4096,512]{1,0:T(8,128)} async-done(((f32[512,512]{1,0:T(8,128)}), f32[4096,512]{1,0:T(8,128)}) %all-gather.19.cloned.1.call-update) | async-done | bytes 8388624 | tf_op jit(solution)/shard_map/all_gather | solution.py:14
  1140.2 11.7 cholesky.358
  1152.1 9.8 custom-call.31
  1162.6 12.1 cholesky.377
  1176.0 9.8 custom-call.32
  1186.5 11.7 cholesky.398
  1198.9 9.8 custom-call.33
  1209.3 11.9 cholesky.415
  1233.7 39.3 %custom-call.34 = f32[4,128,128]{1,2,0:T(8,128)S(1)} custom-call(f32[4,128,128]{2,1,0:T(8,128)S(1)} %get-tuple-element.22), custom_call_target="InvertDiagBlocksLowerTriangular" | custom-call | tf_op jit(solution)/shard_map/jit(_solve_triangular)/triangular_solve | solution.py:44
  1300.3 341.3 %all-gather.21.cloned.1.call-done = f32[32768,512]{1,0:T(8,128)} async-done(((f32[2048,512]{1,0:T(8,128)}), f32[32768,512]{1,0:T(8,128)}) %all-gather.21.cloned.1.call-update) | async-done | bytes 67108880 | tf_op jit(solution)/shard_map/all_gather | solution.py:14
  1641.6 23.1 %reduce_sum.124 = f32[2048,512]{1,0:T(8,128)} reduce(f32[16,2048,512]{2,1,0:T(8,128)} %bitcast.49, f32[]{:T(128)} %constant.221.clone.1), dimensions={0}, to_apply=%region_18.21 | reduce | flops 15728640 | bytes 71303168 | tf_op jit(solution)/shard_map/reduce_sum | solution.py:14
  1667.7 89.2 %all-gather.23.cloned.1.call-done = bf16[8192,512]{1,0:T(8,128)(2,1)} async-done(((bf16[1024,512]{1,0:T(8,128)(2,1)}), bf16[8192,512]{1,0:T(8,128)(2,1)}) %all-gather.23.cloned.1.call-update) | async-done | bytes 8388624 | tf_op jit(solution)/shard_map/all_gather | solution.py:14
  1762.1 15.7 subtract_select_fusion
  (186 shorter events, 206.4 us)
Async XLA Ops:
  26.9 64.2 %all-to-all-start = ((bf16[16,256,512]{2,1,0:T(8,128)(2,1)}), bf16[16,256,512]{2,1,0:T(8,128)(2,1)}, u32[]{:S(2)}, u32[]{:S(2)}) async-start(bf16[16,256,512]{2,1,0:T(8,128)(2,1)} %copy.54), calls=%async_computation | async-start | bytes 8388608 | tf_op jit(solution)/shard_map/all_to_all | solution.py:73
  109.1 99.7 %all-to-all-start.1 = ((bf16[8,1024,512]{2,1,0:T(8,128)(2,1)}), bf16[8,1024,512]{2,1,0:T(8,128)(2,1)}, u32[]{:S(2)}, u32[]{:S(2)}) async-start(bf16[8,1024,512]{2,1,0:T(8,128)(2,1)} %copy.56), calls=%async_computation.1 | async-start | bytes 16777216 | tf_op jit(solution)/shard_map/all_to_all | solution.py:80
  114.1 282.8 %all-gather.13.cloned.1.call-start = ((), (), s32[]{:S(2)}) async-start(), calls=%async_computation.2 | async-start | bytes 9437184 | tf_op jit(solution)/shard_map/all_gather | solution.py:14
  116.2 5.5 copy-start.12
  252.8 9.0 slice-start
  252.8 8.9 slice-start.1
  269.2 3.2 copy-start.1
  273.5 628.9 %all-gather.15.cloned.1.call-start = ((), (), s32[]{:S(2)}) async-start(), calls=%async_computation.3 | async-start | bytes 71303168 | tf_op jit(solution)/shard_map/all_gather | solution.py:14
  494.3 45.9 %copy-start.10 = (f32[512,512]{1,0:T(8,128)}, f32[512,512]{1,0:T(8,128)S(1)}, u32[]{:S(2)}) copy-start(f32[512,512]{1,0:T(8,128)S(1)} %get-tuple-element.201) | copy-start | bytes 3145732
  533.6 6.6 copy-start.4
  553.7 2.6 copy-start.6
  555.0 2.3 copy-start.8
  561.0 456.6 %all-gather.17.cloned.1.call-start = ((), (), s32[]{:S(2)}) async-start(), calls=%async_computation.4 | async-start | bytes 9437184 | tf_op jit(solution)/shard_map/all_gather | solution.py:14
  928.4 206.7 %all-gather.19.cloned.1.call-start = ((), (), s32[]{:S(2)}) async-start(), calls=%async_computation.5 | async-start | bytes 9437184 | tf_op jit(solution)/shard_map/all_gather | solution.py:14
  1022.9 15.7 copy-start.3
  1039.9 3.2 copy-start
  1044.3 597.3 %all-gather.21.cloned.1.call-start = ((), (), s32[]{:S(2)}) async-start(), calls=%async_computation.6 | async-start | bytes 71303168 | tf_op jit(solution)/shard_map/all_gather | solution.py:14
  1233.7 45.9 %copy-start.11 = (f32[512,512]{1,0:T(8,128)}, f32[512,512]{1,0:T(8,128)S(1)}, u32[]{:S(2)}) copy-start(f32[512,512]{1,0:T(8,128)S(1)} %get-tuple-element.202) | copy-start | bytes 3145732
  1273.0 6.6 copy-start.5
  1292.8 2.6 copy-start.7
  1294.2 2.3 copy-start.9
  1300.2 456.6 %all-gather.23.cloned.1.call-start = ((), (), s32[]{:S(2)}) async-start(), calls=%async_computation.7 | async-start | bytes 9437184 | tf_op jit(solution)/shard_map/all_gather | solution.py:14
  1762.1 15.7 copy-start.2
Sparse Core Ops, SparseCore 0:
  273.7 123.1 all-gather.12
  561.2 341.2 all-gather.14
  928.5 89.0 all-gather.16
  1044.4 90.6 all-gather.18
  1300.3 341.2 all-gather.20
  1667.8 89.0 all-gather.22
